TPU v7x, 32 devices: a whole 2x2x4 slice. The times are simulated.
32 devices in a mesh: dp: 8 (over y, x, core), tensor: 4 (over z).
Axes of the slice: x: 2, y: 2, z: 4, core: 2. Of those that a mesh axis runs over, the one named last changes fastest.
Arguments:
- tokens: bfloat16 [8192, 2048], P(('dp', 'tensor')), may hold values from -6 to 6
- cotangent: bfloat16 [8192, 2048], P(('dp', 'tensor')), may hold values from -6 to 6
- norm_gains: float32 [2, 2048], replicated, may hold values from 0.1 to 1.9
- norm_shifts: float32 [2, 2048], replicated, may hold values from -4 to 4
- query_key_value_weight: bfloat16 [2048, 3, 2048], P(None, None, 'tensor'), may hold values from -0.125 to 0.125
- b_qv: float32 [2, 2048], P(None, 'tensor'), may hold values from -4 to 4
- output_weight: bfloat16 [2048, 2048], P('tensor'), may hold values from -0.375 to 0.375
- output_bias_vector: float32 [2048], replicated, may hold values from -4 to 4
- up_weight: bfloat16 [2048, 8192], P(None, 'tensor'), may hold values from -0.125 to 0.125
- b_up: float32 [8192], P('tensor'), may hold values from -4 to 4
- down_weight: bfloat16 [8192, 2048], P('tensor'), may hold values from -0.0625 to 0.0625
- down_bias_vector: float32 [2048], replicated, may hold values from -4 to 4
- adapter_query_key_value_input: bfloat16 [8, 16, 2048], replicated, may hold values from -0.125 to 0.125
- qkv_out: bfloat16 [8, 16, 3, 2048], P(None, None, None, 'tensor'), may hold values from -1.5 to 1.5
- adapter_output_input: bfloat16 [8, 16, 2048], P(None, None, 'tensor'), may hold values from -0.375 to 0.375
- adapter_output_output: bfloat16 [8, 16, 2048], replicated, may hold values from -1.5 to 1.5
- adapter_up_input: bfloat16 [8, 16, 2048], replicated, may hold values from -0.125 to 0.125
- up_out: bfloat16 [8, 16, 8192], P(None, None, 'tensor'), may hold values from -1.5 to 1.5
- down_in: bfloat16 [8, 16, 8192], P(None, None, 'tensor'), may hold values from -0.0625 to 0.0625
- adapter_down_output: bfloat16 [8, 16, 2048], replicated, may hold values from -1.5 to 1.5
- offsets: int32 [8, 2], P('dp'), may hold values from 0 to 768, as said below
- adapter_ids: int32 [8, 4], P('dp'), may hold values from 0 to 7
Outputs:
- out: bfloat16 [8192, 2048], P(('dp', 'tensor'))
- in_grad: bfloat16 [8192, 2048], P(('dp', 'tensor'))
- g_qkv_in: float32 [8, 16, 2048], replicated
- g_qkv_out: float32 [8, 16, 3, 2048], P(None, None, None, 'tensor')
- g_out_in: float32 [8, 16, 2048], P(None, None, 'tensor')
- g_out_out: float32 [8, 16, 2048], replicated
- g_up_in: float32 [8, 16, 2048], replicated
- g_up_out: float32 [8, 16, 8192], P(None, None, 'tensor')
- g_down_in: float32 [8, 16, 8192], P(None, None, 'tensor')
- g_down_out: float32 [8, 16, 2048], replicated
Inputs may be any that keep to these rules, and one draw needn't show every extreme that they name: For every sequence s, offsets[s, 0] + 256 <= offsets[s, 1]: the two pieces of 256 positions lie inside the sequence and don't intersect.
All inputs are finite; a program needn't handle non-finite values.
Results may differ from a plain program's by a relative error of at most 0.02.
Values may be sent and summed in bfloat16 or wider, within the bound.
A program may use at most 192 MiB of HBM per device.

v0:
```python
import math
import jax
import jax.numpy as jnp
from jax import lax
from jax.sharding import PartitionSpec as P

HEADS = 16
HEAD_DIM = 128
PIECE = 256
EPS = 1e-05
GELU_C = 0.7978845608028654
GELU_K = 0.044715
NEGATIVE = -1e30
EXACT_MODE = lax.Precision.HIGHEST


def layer_norm(values, gain_row, shift_row):
    centre = values - jnp.mean(values, axis=-1, keepdims=True)
    spread = jnp.mean(centre * centre, axis=-1, keepdims=True)
    inverse = lax.rsqrt(spread + EPS)
    scaled = centre * inverse
    return (scaled * gain_row + shift_row, scaled, inverse)


def norm_back(grad_rows, scaled, inverse, gain_row):
    inner_grad = grad_rows * gain_row
    first_mean = jnp.mean(inner_grad, axis=-1, keepdims=True)
    second_mean = jnp.mean(inner_grad * scaled, axis=-1, keepdims=True)
    return inverse * (inner_grad - first_mean - scaled * second_mean)


def gelu_parts(values):
    cubic = GELU_K * values * values * values
    tangent = jnp.tanh(GELU_C * (values + cubic))
    gelu_value = 0.5 * values * (1.0 + tangent)
    gelu_slope = 0.5 * (1.0 + tangent) + 0.5 * values * (1.0 - tangent * tangent) * GELU_C * (
        1.0 + 3.0 * GELU_K * values * values
    )
    return (gelu_value, gelu_slope)


def dot_transposed(left, right):
    return lax.dot_general(
        left, right, (((1,), (1,)), ((), ())), preferred_element_type=jnp.float32
    )


def choose(adapter_table, indicator_matrix):
    picked = jnp.einsum(
        "ge,erm->grm", indicator_matrix, adapter_table, preferred_element_type=jnp.float32
    )
    return picked.astype(jnp.bfloat16)


def low_rank_down(activations, chosen):
    shaped = activations.reshape(chosen.shape[0], -1, activations.shape[-1])
    return jnp.einsum("glm,grm->glr", shaped, chosen, preferred_element_type=jnp.float32)


def low_rank_upward(rank_rows, chosen):
    product = jnp.einsum(
        "glr,grm->glm", rank_rows, chosen.astype(jnp.float32), precision=EXACT_MODE
    )
    return product.reshape(-1, product.shape[-1])


def rank_grad(rank_rows, activations):
    shaped = activations.reshape(rank_rows.shape[0], -1, activations.shape[-1]).astype(jnp.float32)
    return jnp.einsum("glr,glm->grm", rank_rows, shaped, precision=EXACT_MODE)


def to_tables(per_sequence, indicator_matrix):
    return jnp.einsum("ge,grm->erm", indicator_matrix, per_sequence, precision=EXACT_MODE)


def block_scores(query_rows, key_rows, pieces, slopes, first_row):
    rows_here = query_rows.shape[1]
    length = key_rows.shape[1]
    keys_at = jnp.arange(length, dtype=jnp.int32)
    query_at = first_row + jnp.arange(rows_here, dtype=jnp.int32)
    scaling = 1.0 / math.sqrt(key_rows.shape[3])
    scores = (
        jnp.einsum("gqhd,gkhd->ghqk", query_rows, key_rows, preferred_element_type=jnp.float32)
        * scaling
    )
    distance = jnp.abs(query_at[:, None] - keys_at[None, :]).astype(jnp.float32)
    scores = scores - slopes[None, :, None, None] * distance[None, None]
    piece_rows = pieces[:, first_row : first_row + rows_here]
    allowed = (keys_at[None, None, :] <= query_at[None, :, None]) | (
        piece_rows[:, :, None] == pieces[:, None, :]
    ) & (piece_rows[:, :, None] > 0)
    return jnp.where(allowed[:, None], scores, NEGATIVE)


def attend(queries, key_rows, values, pieces, slopes):
    length = queries.shape[1]
    block_rows = min(512, length)
    contexts = []
    log_sums = []
    for first_row in range(0, length, block_rows):
        scores = block_scores(
            queries[:, first_row : first_row + block_rows], key_rows, pieces, slopes, first_row
        )
        row_peak = jnp.max(scores, axis=-1, keepdims=True)
        exponent = jnp.exp(scores - row_peak)
        total_sum = jnp.sum(exponent, axis=-1, keepdims=True)
        weights = (exponent / total_sum).astype(jnp.bfloat16)
        contexts.append(
            jnp.einsum("ghqk,gkhd->gqhd", weights, values, preferred_element_type=jnp.float32)
        )
        log_sums.append(row_peak + jnp.log(total_sum))
    return (jnp.concatenate(contexts, 1), jnp.concatenate(log_sums, 2))


def attend_back(queries, key_rows, values, pieces, slopes, log_sums, grad_context):
    length = queries.shape[1]
    block_rows = min(512, length)
    scaling = 1.0 / math.sqrt(key_rows.shape[3])
    grad_queries = []
    grad_keys = jnp.zeros(key_rows.shape, jnp.float32)
    grad_values = jnp.zeros(values.shape, jnp.float32)
    for first_row in range(0, length, block_rows):
        query_rows = queries[:, first_row : first_row + block_rows]
        grad_rows = grad_context[:, first_row : first_row + block_rows]
        scores = block_scores(query_rows, key_rows, pieces, slopes, first_row)
        probability = jnp.exp(scores - log_sums[:, :, first_row : first_row + block_rows])
        grad_values = grad_values + jnp.einsum(
            "ghqk,gqhd->gkhd",
            probability.astype(jnp.bfloat16),
            grad_rows,
            preferred_element_type=jnp.float32,
        )
        grad_probs = jnp.einsum(
            "gqhd,gkhd->ghqk", grad_rows, values, preferred_element_type=jnp.float32
        )
        inner_sum = jnp.sum(probability * grad_probs, axis=-1, keepdims=True)
        grad_scores = (probability * (grad_probs - inner_sum)).astype(jnp.bfloat16)
        grad_queries.append(
            jnp.einsum("ghqk,gkhd->gqhd", grad_scores, key_rows, preferred_element_type=jnp.float32)
            * scaling
        )
        grad_keys = (
            grad_keys
            + jnp.einsum(
                "ghqk,gqhd->gkhd", grad_scores, query_rows, preferred_element_type=jnp.float32
            )
            * scaling
        )
    return (jnp.concatenate(grad_queries, 1), grad_keys, grad_values)


def body(
    tokens,
    cotangent,
    norm_gains,
    norm_shifts,
    query_key_value_weight,
    b_qv,
    output_weight,
    output_bias_vector,
    up_weight,
    b_up,
    down_weight,
    down_bias_vector,
    adapter_query_key_value_input,
    qkv_out,
    adapter_output_input,
    adapter_output_output,
    adapter_up_input,
    up_out,
    down_in,
    adapter_down_output,
    offsets,
    adapter_ids,
):
    row_count = tokens.shape[0]
    model_width = tokens.shape[1]
    position = lax.axis_index("tensor")
    seq_count = offsets.shape[0]
    full_rows = row_count * lax.axis_size("tensor")
    length = full_rows // seq_count
    local_width = query_key_value_weight.shape[2]
    local_heads = local_width // HEAD_DIM
    table_count = adapter_query_key_value_input.shape[0]
    indicator_matrix = (
        adapter_ids[:, :, None] == jnp.arange(table_count, dtype=jnp.int32)[None, None, :]
    ).astype(jnp.float32)
    one_low = indicator_matrix.astype(jnp.bfloat16)
    chosen_qkv_in = choose(adapter_query_key_value_input, one_low[:, 0])
    chosen_qkv_out = choose(
        qkv_out.reshape(table_count, qkv_out.shape[1], 3 * local_width), one_low[:, 0]
    )
    chosen_out_in = choose(adapter_output_input, one_low[:, 1])
    chosen_out_out = choose(adapter_output_output, one_low[:, 1])
    chosen_up_in = choose(adapter_up_input, one_low[:, 2])
    chosen_up_out = choose(up_out, one_low[:, 2])
    chosen_down_in = choose(down_in, one_low[:, 3])
    chosen_down_out = choose(adapter_down_output, one_low[:, 3])
    where_at = jnp.arange(length, dtype=jnp.int32)
    first_piece = (
        (where_at[None, :] >= offsets[:, 0:1]) & (where_at[None, :] < offsets[:, 0:1] + PIECE)
    ).astype(jnp.int32)
    second_piece = (
        (where_at[None, :] >= offsets[:, 1:2]) & (where_at[None, :] < offsets[:, 1:2] + PIECE)
    ).astype(jnp.int32)
    pieces = first_piece + 2 * second_piece
    head_ids = (position * local_heads + jnp.arange(local_heads, dtype=jnp.int32)).astype(
        jnp.float32
    )
    slopes = jnp.exp2(-8.0 * (head_ids + 1.0) / HEADS)
    qkv_flat = query_key_value_weight.reshape(model_width, 3 * local_width)
    qkv_bias = jnp.concatenate([b_qv[0], jnp.zeros_like(b_qv[0]), b_qv[1]])
    inputs = tokens.astype(jnp.float32)
    normed_local, scaled_first, inverse_first = layer_norm(inputs, norm_gains[0], norm_shifts[0])
    sent_in = normed_local.astype(jnp.bfloat16)
    arrived = lax.all_gather(sent_in, "tensor", axis=0, tiled=True)
    low_rank_query_key_value = low_rank_down(arrived, chosen_qkv_in)
    projection_result = (
        jnp.dot(arrived, qkv_flat, preferred_element_type=jnp.float32)
        + low_rank_upward(low_rank_query_key_value, chosen_qkv_out)
        + qkv_bias
    )
    projection_result = projection_result.astype(jnp.bfloat16).reshape(
        seq_count, length, 3, local_heads, HEAD_DIM
    )
    queries = projection_result[:, :, 0]
    key_rows = projection_result[:, :, 1]
    values = projection_result[:, :, 2]
    attended_context, log_sums = attend(queries, key_rows, values, pieces, slopes)
    attended_context = attended_context.astype(jnp.bfloat16).reshape(full_rows, local_width)
    rank_ctx = low_rank_down(attended_context, chosen_out_in)
    ctx_term = low_rank_upward(rank_ctx, chosen_out_out)
    row_block = attended_context
    side_path = lax.psum_scatter(
        (jnp.dot(row_block, output_weight, preferred_element_type=jnp.float32) + ctx_term).astype(
            jnp.bfloat16
        ),
        "tensor",
        scatter_dimension=0,
        tiled=True,
    ).astype(jnp.float32)
    middle = inputs + (side_path + output_bias_vector)
    normed_mid_local, scaled_second, inverse_second = layer_norm(
        middle, norm_gains[1], norm_shifts[1]
    )
    normalized_middle = lax.all_gather(
        normed_mid_local.astype(jnp.bfloat16), "tensor", axis=0, tiled=True
    )
    rank_upper = low_rank_down(normalized_middle, chosen_up_in)
    gate_input_rows = (
        jnp.dot(normalized_middle, up_weight, preferred_element_type=jnp.float32)
        + low_rank_upward(rank_upper, chosen_up_out)
        + b_up
    )
    hidden_value, hidden_slope = gelu_parts(gate_input_rows)
    hidden_rows = hidden_value.astype(jnp.bfloat16)
    rank_lower = low_rank_down(hidden_rows, chosen_down_in)
    lower_term = low_rank_upward(rank_lower, chosen_down_out)
    row_block = hidden_rows
    mlp_part = lax.psum_scatter(
        (jnp.dot(row_block, down_weight, preferred_element_type=jnp.float32) + lower_term).astype(
            jnp.bfloat16
        ),
        "tensor",
        scatter_dimension=0,
        tiled=True,
    ).astype(jnp.float32)
    result = (middle + (mlp_part + down_bias_vector)).astype(jnp.bfloat16)
    grad_out = lax.all_gather(cotangent, "tensor", axis=0, tiled=True)
    grad_rank_lower = low_rank_down(grad_out, chosen_down_out)
    table_down_out = rank_grad(rank_lower, grad_out)
    table_down_in = rank_grad(grad_rank_lower, hidden_rows)
    grad_hidden = dot_transposed(grad_out, down_weight) + low_rank_upward(
        grad_rank_lower, chosen_down_in
    )
    grad_gate = (grad_hidden * hidden_slope).astype(jnp.bfloat16)
    grad_rank_upper = low_rank_down(grad_gate, chosen_up_out)
    table_up_out = rank_grad(rank_upper, grad_gate)
    table_up_in = rank_grad(grad_rank_upper, normalized_middle)
    upper_back = low_rank_upward(grad_rank_upper, chosen_up_in)
    row_block = grad_gate
    grad_mid_norm = lax.psum_scatter(
        (dot_transposed(row_block, up_weight) + upper_back).astype(jnp.bfloat16),
        "tensor",
        scatter_dimension=0,
        tiled=True,
    ).astype(jnp.float32)
    grad_middle = cotangent.astype(jnp.float32) + norm_back(
        grad_mid_norm, scaled_second, inverse_second, norm_gains[1]
    )
    grad_mid_low = lax.all_gather(grad_middle.astype(jnp.bfloat16), "tensor", axis=0, tiled=True)
    grad_rank_ctx = low_rank_down(grad_mid_low, chosen_out_out)
    table_out_out = rank_grad(rank_ctx, grad_mid_low)
    table_out_in = rank_grad(grad_rank_ctx, attended_context)
    grad_context = dot_transposed(grad_mid_low, output_weight) + low_rank_upward(
        grad_rank_ctx, chosen_out_in
    )
    grad_context = grad_context.astype(jnp.bfloat16).reshape(
        seq_count, length, local_heads, HEAD_DIM
    )
    grad_queries, grad_keys, grad_values = attend_back(
        queries, key_rows, values, pieces, slopes, log_sums, grad_context
    )
    grad_proj = (
        jnp.stack([grad_queries, grad_keys, grad_values], 2)
        .astype(jnp.bfloat16)
        .reshape(full_rows, 3 * local_width)
    )
    grad_rank_qkv = low_rank_down(grad_proj, chosen_qkv_out)
    table_qkv_out = rank_grad(low_rank_query_key_value, grad_proj)
    table_qkv_in = rank_grad(grad_rank_qkv, arrived)
    first_back = low_rank_upward(grad_rank_qkv, chosen_qkv_in)
    row_block = grad_proj
    grad_first = lax.psum_scatter(
        (dot_transposed(row_block, qkv_flat) + first_back).astype(jnp.bfloat16),
        "tensor",
        scatter_dimension=0,
        tiled=True,
    ).astype(jnp.float32)
    grad_tokens = (
        grad_middle + norm_back(grad_first, scaled_first, inverse_first, norm_gains[0])
    ).astype(jnp.bfloat16)
    shared = lax.psum(
        (
            to_tables(table_qkv_in, indicator_matrix[:, 0]),
            to_tables(table_out_out, indicator_matrix[:, 1]),
            to_tables(table_up_in, indicator_matrix[:, 2]),
            to_tables(table_down_out, indicator_matrix[:, 3]),
        ),
        ("dp", "tensor"),
    )
    owned_sums = (
        lax.psum(
            to_tables(table_qkv_out, indicator_matrix[:, 0])
            .reshape(qkv_out.shape)
            .astype(jnp.bfloat16),
            "dp",
        ).astype(jnp.float32),
        lax.psum(to_tables(table_out_in, indicator_matrix[:, 1]).astype(jnp.bfloat16), "dp").astype(
            jnp.float32
        ),
        lax.psum(to_tables(table_up_out, indicator_matrix[:, 2]).astype(jnp.bfloat16), "dp").astype(
            jnp.float32
        ),
        lax.psum(
            to_tables(table_down_in, indicator_matrix[:, 3]).astype(jnp.bfloat16), "dp"
        ).astype(jnp.float32),
    )
    return (
        result,
        grad_tokens,
        shared[0],
        owned_sums[0],
        owned_sums[1],
        shared[1],
        shared[2],
        owned_sums[2],
        owned_sums[3],
        shared[3],
    )


def solution(mesh):
    placed = (
        P(("dp", "tensor"), None),
        P(("dp", "tensor"), None),
        P(),
        P(),
        P(None, None, "tensor"),
        P(None, "tensor"),
        P("tensor", None),
        P(),
        P(None, "tensor"),
        P("tensor"),
        P("tensor", None),
        P(),
        P(),
        P(None, None, None, "tensor"),
        P(None, None, "tensor"),
        P(),
        P(),
        P(None, None, "tensor"),
        P(None, None, "tensor"),
        P(),
        P("dp", None),
        P("dp", None),
    )
    return jax.shard_map(
        body,
        mesh=mesh,
        in_specs=placed,
        out_specs=(
            P(("dp", "tensor"), None),
            P(("dp", "tensor"), None),
            P(),
            P(None, None, None, "tensor"),
            P(None, None, "tensor"),
            P(),
            P(),
            P(None, None, "tensor"),
            P(None, None, "tensor"),
            P(),
        ),
        check_vma=False,
    )
```

profile of v0, /device:TPU:0, one launch (start us, length us, event | category | flops | bytes accessed | tf_op | source)
XLA Modules:
  0.0 1041.3 jit_solution(12768031125403590012)
XLA Ops:
  17.7 9.0 copy.45
  38.1 60.4 %all-gather.5.cloned.1.call-done = bf16[1024,2048]{1,0:T(8,128)(2,1)} async-done(((bf16[256,2048]{1,0:T(8,128)(2,1)}), bf16[1024,2048]{1,0:T(8,128)(2,1)}) %all-gather.5.cloned.1.call-update) | async-done | bytes 4194320 | tf_op jit(solution)/shard_map/all_gather | solution.py:216
  102.0 8.8 fusion.112
  115.4 6.2 reshape.957
  151.7 5.6 add_convert_fusion.3
  158.2 74.7 %reduce-scatter.5.cloned.1.call-done = bf16[256,2048]{1,0:T(8,128)(2,1)} async-done(((bf16[1024,2048]{1,0:T(8,128)(2,1)}), bf16[256,2048]{1,0:T(8,128)(2,1)}) %reduce-scatter.5.cloned.1.call-update) | async-done | bytes 1048592 | tf_op jit(solution)/shard_map/reduce_scatter | solution.py:234
  245.7 70.1 %all-gather.9.cloned.1.call-done = bf16[1024,2048]{1,0:T(8,128)(2,1)} async-done(((bf16[256,2048]{1,0:T(8,128)(2,1)}), bf16[1024,2048]{1,0:T(8,128)(2,1)}) %all-gather.9.cloned.1.call-update) | async-done | bytes 4194320 | tf_op jit(solution)/shard_map/all_gather | solution.py:269
  320.0 13.4 %fusion.115 = f32[1024,2048]{1,0:T(8,128)} fusion(bf16[1024,2048]{1,0:T(8,128)(2,1)S(1)} %copy-done.14, bf16[2048,2048]{1,0:T(8,128)(2,1)} %param.32), kind=kOutput, calls=%fused_computation.205 | convolution fusion | flops 8589934592 | bytes 20971520 | tf_op jit(solution)/shard_map/dot_general | solution.py:43
  333.4 63.8 %all-gather.7.cloned.1.call-done = bf16[1024,2048]{1,0:T(8,128)(2,1)} async-done(((bf16[256,2048]{1,0:T(8,128)(2,1)}), bf16[1024,2048]{1,0:T(8,128)(2,1)}) %all-gather.7.cloned.1.call-update) | async-done | bytes 4194320 | tf_op jit(solution)/shard_map/all_gather | solution.py:246
  400.8 13.3 %fusion.113 = f32[1024,2048]{1,0:T(8,128)} fusion(bf16[1024,2048]{1,0:T(8,128)(2,1)S(1)} %copy-done.9, bf16[2048,2048]{1,0:T(8,128)(2,1)} %param.30), kind=kOutput, calls=%fused_computation.203 | convolution fusion | flops 8589934592 | bytes 20971520 | tf_op jit(solution)/shard_map/dot_general | solution.py:251
  414.1 10.2 multiply_convert_fusion.2
  424.3 11.1 %fusion.6 = bf16[1024,2048]{1,0:T(8,128)(2,1)S(1)} fusion(f32[1024,2048]{1,0:T(8,128)S(1)} %get-tuple-element.55, f32[1024,2048]{1,0:T(8,128)} %fusion.115, f32[16,1024]{1,0:T(8,128)S(1)} %copy-done.49, bf16[1,16,2048]{2,0,1:T(2,128)(2,1)S(1)} %copy-done.45), kind=kOutput, calls=%fused_computation.8 | convolution fusion | flops 444596224 | bytes 21102592 | tf_op jit(solution)/shard_map/glr,grm->glm/dot_general | solution.py:61
  436.7 8.8 fusion.116
  454.8 11.9 %fusion.114 = f32[1024,2048]{1,0:T(8,128)S(1)} fusion(bf16[1024,2048]{1,0:T(8,128)(2,1)S(1)} %copy-done.13, bf16[2048,2048]{1,0:T(8,128)(2,1)} %param.32), kind=kOutput, calls=%fused_computation.204 | convolution fusion | flops 8589934592 | bytes 20971520 | tf_op jit(solution)/shard_map/dot_general | solution.py:261
  466.7 5.5 add_convert_fusion.2
  472.3 54.0 %reduce-scatter.9.cloned.1.call-done = bf16[256,2048]{1,0:T(8,128)(2,1)} async-done(((bf16[1024,2048]{1,0:T(8,128)(2,1)}), bf16[256,2048]{1,0:T(8,128)(2,1)}) %reduce-scatter.9.cloned.1.call-update) | async-done | bytes 1048592 | tf_op jit(solution)/shard_map/reduce_scatter | solution.py:282
  528.7 77.0 %reduce-scatter.7.cloned.1.call-done = bf16[256,2048]{1,0:T(8,128)(2,1)} async-done(((bf16[1024,2048]{1,0:T(8,128)(2,1)}), bf16[256,2048]{1,0:T(8,128)(2,1)}) %reduce-scatter.7.cloned.1.call-update) | async-done | bytes 1048592 | tf_op jit(solution)/shard_map/reduce_scatter | solution.py:260
  605.7 5.7 fusion.103
  626.6 66.4 %all-gather.11.cloned.1.call-done = bf16[1024,2048]{1,0:T(8,128)(2,1)} async-done(((bf16[256,2048]{1,0:T(8,128)(2,1)}), bf16[1024,2048]{1,0:T(8,128)(2,1)}) %all-gather.11.cloned.1.call-update) | async-done | bytes 4194320 | tf_op jit(solution)/shard_map/all_gather | solution.py:291
  728.4 9.5 fusion.118
  742.0 7.7 add_convert_fusion
  758.7 38.8 %all-reduce.7.cloned.1.call-done = (bf16[8,16,3,512]{3,1,2,0:T(8,128)(2,1)}, bf16[8,16,512]{2,1,0:T(8,128)(2,1)}, bf16[8,16,2048]{2,1,0:T(8,128)(2,1)}, bf16[8,16,2048]{2,1,0:T(8,128)(2,1)}) async-done(((bf16[8,16,3,512]{3,1,2,0:T(8,128)(2,1)}, bf16[8,16,512]{2,1,0:T(8,128)(2,1)}, bf16[8,16,2048]{2,1,0:T(8,128)(2,1)}, bf16[8,16,2048]{2,1,0:T(8,128)(2,1)}), (bf16[8,16,3,512]{3,1,2,0:T(8,128)(2,1)}, ...) | async-done | bytes 1572880 | tf_op jit(solution)/shard_map/psum | solution.py:333
  805.4 70.6 %reduce-scatter.11.cloned.1.call-done = bf16[256,2048]{1,0:T(8,128)(2,1)} async-done(((bf16[1024,2048]{1,0:T(8,128)(2,1)}), bf16[256,2048]{1,0:T(8,128)(2,1)}) %reduce-scatter.11.cloned.1.call-update) | async-done | bytes 1048592 | tf_op jit(solution)/shard_map/reduce_scatter | solution.py:314
  881.7 145.7 %all-reduce.5.cloned.1.call-done = (f32[8,16,2048]{2,1,0:T(8,128)}, f32[8,16,2048]{2,1,0:T(8,128)}, f32[8,16,2048]{2,1,0:T(8,128)}, f32[8,16,2048]{2,1,0:T(8,128)}) async-done(((f32[8,16,2048]{2,1,0:T(8,128)}, f32[8,16,2048]{2,1,0:T(8,128)}, f32[8,16,2048]{2,1,0:T(8,128)}, f32[8,16,2048]{2,1,0:T(8,128)}), (f32[8,16,2048]{2,1,0:T(8,128)}, f32[8,16,2048]{2,1,0:T(8,128)}, f32[8,16,2048]{2,1,0:T(8,128)}, ...) | async-done | bytes 4194320 | tf_op jit(solution)/shard_map/psum | solution.py:323
  (304 shorter events, 176.0 us)
Async XLA Ops:
  7.2 142.1 %copy-start = (bf16[512,2048]{1,0:T(8,128)(2,1)S(1)}, bf16[512,2048]{1,0:T(8,128)(2,1)}, u32[]{:S(2)}) copy-start(bf16[512,2048]{1,0:T(8,128)(2,1)} %param.28) | copy-start | bytes 6291460
  7.2 91.3 %all-gather.5.cloned.1.call-start = ((), (), s32[]{:S(2)}) async-start(), calls=%async_computation.4 | async-start | bytes 5242880 | tf_op jit(solution)/shard_map/all_gather | solution.py:216
  14.9 218.0 %reduce-scatter.5.cloned.1.call-start = ((), (), s32[]{:S(2)}) async-start(), calls=%async_computation.5 | async-start | bytes 5242880 | tf_op jit(solution)/shard_map/reduce_scatter | solution.py:234
  31.6 206.5 %copy-start.55 = (bf16[1,4,8]{2,1,0:T(4,128)(2,1)}, bf16[1,4,8]{2,1,0:T(4,128)(2,1)S(1)}, u32[]{:S(2)}) copy-start(bf16[1,4,8]{2,1,0:T(4,128)(2,1)S(1)} %get-tuple-element.47) | copy-start | bytes 196
  31.9 117.1 %copy-start.56 = (bf16[1,16,512]{2,0,1:T(2,128)(2,1)}, bf16[1,16,512]{2,0,1:T(2,128)(2,1)S(1)}, u32[]{:S(2)}) copy-start(bf16[1,16,512]{2,0,1:T(2,128)(2,1)S(1)} %fusion.65) | copy-start | bytes 49156
  32.1 78.7 %copy-start.40 = (bf16[1,16,1536]{2,0,1:T(2,128)(2,1)}, bf16[1,16,1536]{2,0,1:T(2,128)(2,1)S(1)}, u32[]{:S(2)}) copy-start(bf16[1,16,1536]{2,0,1:T(2,128)(2,1)S(1)} %fusion.89) | copy-start | bytes 147460
  34.1 67.9 %copy-start.34 = (bf16[1,16,2048]{2,0,1:T(2,128)(2,1)}, bf16[1,16,2048]{2,0,1:T(2,128)(2,1)S(1)}, u32[]{:S(2)}) copy-start(bf16[1,16,2048]{2,0,1:T(2,128)(2,1)S(1)} %fusion.59) | copy-start | bytes 196612
  157.3 75.5 %copy-start.3 = (bf16[256,2048]{1,0:T(8,128)(2,1)S(1)}, bf16[256,2048]{1,0:T(8,128)(2,1)}, u32[]{:S(2)}) copy-start(bf16[256,2048]{1,0:T(8,128)(2,1)} %param.22) | copy-start | bytes 3145732
  157.3 75.5 %copy-start.51 = (f32[2048]{0:T(1024)S(1)}, f32[2048]{0:T(1024)}, u32[]{:S(2)}) copy-start(f32[2048]{0:T(1024)} %param.29) | copy-start | bytes 24580
  157.4 158.4 %all-gather.9.cloned.1.call-start = ((), (), s32[]{:S(2)}) async-start(), calls=%async_computation.8 | async-start | bytes 5242880 | tf_op jit(solution)/shard_map/all_gather | solution.py:269
  158.1 239.1 %all-gather.7.cloned.1.call-start = ((), (), s32[]{:S(2)}) async-start(), calls=%async_computation.6 | async-start | bytes 5242880 | tf_op jit(solution)/shard_map/all_gather | solution.py:246
  238.1 288.2 %reduce-scatter.9.cloned.1.call-start = ((), (), s32[]{:S(2)}) async-start(), calls=%async_computation.9 | async-start | bytes 5242880 | tf_op jit(solution)/shard_map/reduce_scatter | solution.py:282
  245.7 151.5 %copy-start.36 = (bf16[1,16,2048]{2,0,1:T(2,128)(2,1)}, bf16[1,16,2048]{2,0,1:T(2,128)(2,1)S(1)}, u32[]{:S(2)}) copy-start(bf16[1,16,2048]{2,0,1:T(2,128)(2,1)S(1)} %fusion.55) | copy-start | bytes 196612
  450.9 154.9 %reduce-scatter.7.cloned.1.call-start = ((), (), s32[]{:S(2)}) async-start(), calls=%async_computation.7 | async-start | bytes 5242880 | tf_op jit(solution)/shard_map/reduce_scatter | solution.py:260
  472.2 54.1 %copy-start.69 = (f32[256]{0:T(256)S(1)}, f32[256]{0:T(256)}, u32[]{:S(2)}) copy-start(f32[256]{0:T(256)} %copy-done.68) | copy-start | bytes 3076
  472.2 133.5 %copy-start.70 = (f32[2048]{0:T(1024)S(1)}, f32[2048]{0:T(1024)}, u32[]{:S(2)}) copy-start(f32[2048]{0:T(1024)} %param.33) | copy-start | bytes 24580
  472.2 220.7 %all-gather.11.cloned.1.call-start = ((), (), s32[]{:S(2)}) async-start(), calls=%async_computation.10 | async-start | bytes 5242880 | tf_op jit(solution)/shard_map/all_gather | solution.py:291
  528.7 85.8 %copy-start.50 = (f32[16,1024]{1,0:T(8,128)S(1)}, f32[16,1024]{1,0:T(8,128)}, u32[]{:S(2)}) copy-start(f32[16,1024]{1,0:T(8,128)} %fusion.74) | copy-start | bytes 196612
  611.5 186.1 %all-reduce.7.cloned.1.call-start = ((), (), s32[]{:S(2)}) async-start(), calls=%async_computation.13 | async-start | bytes 3145728 | tf_op jit(solution)/shard_map/psum | solution.py:333
  739.5 136.5 %reduce-scatter.11.cloned.1.call-start = ((), (), s32[]{:S(2)}) async-start(), calls=%async_computation.11 | async-start | bytes 5242880 | tf_op jit(solution)/shard_map/reduce_scatter | solution.py:314
  749.7 277.6 %all-reduce.5.cloned.1.call-start = ((), (), s32[]{:S(2)}) async-start(), calls=%async_computation.12 | async-start | bytes 8388608 | tf_op jit(solution)/shard_map/psum | solution.py:323
  758.7 117.4 %copy-start.53 = (f32[1,2048]{1,0:T(1,128)S(1)}, f32[1,2048]{1,0:T(1,128)}, u32[]{:S(2)}) copy-start(f32[1,2048]{1,0:T(1,128)} %copy-done.52) | copy-start | bytes 24580
  758.7 117.4 %copy-start.65 = (f32[256]{0:T(256)S(1)}, f32[256]{0:T(256)}, u32[]{:S(2)}) copy-start(f32[256]{0:T(256)} %copy-done.64) | copy-start | bytes 3076
  758.7 117.4 %copy-start.67 = (f32[256]{0:T(256)S(1)}, f32[256]{0:T(256)}, u32[]{:S(2)}) copy-start(f32[256]{0:T(256)} %copy-done.66) | copy-start | bytes 3076
  (75 other events, 536.1 us)
Sparse Core Ops, SparseCore 0:
  15.0 83.4 all-gather.4
  157.5 75.2 reduce-scatter.4
  234.5 81.2 all-gather.8
  317.9 79.2 all-gather.6
  451.0 75.2 reduce-scatter.8
  528.5 77.2 reduce-scatter.6
  611.6 81.2 all-gather.10
  739.7 57.8 all-reduce.6
  799.9 76.1 reduce-scatter.10
  883.9 143.3 all-reduce.4
where the time goes:
time: 1050 us; the launch traced here: 1040 us
  waiting for transfers between devices  722 us (69%)
  matrix products  203 us (19%)
  other arithmetic  58.5 us (6%)
  local copies, waits for them, and re-layouts  39.8 us (4%)
  between operations  17 us (2%)
    psum x1, waiting for transfers between devices, body(): lax.psum((to_tables(table_qkv_in, indicator_matrix[:, 0]), to_tables(tabl...  146 us
    reduce_scatter x1, waiting for transfers between devices, body(): lax.psum_scatter((jnp.dot(row_block, down_weight, preferred_element_type=...  77 us
    reduce_scatter x1, waiting for transfers between devices, body(): lax.psum_scatter((jnp.dot(row_block, output_weight, preferred_element_typ...  74.7 us
    reduce_scatter x1, waiting for transfers between devices, body(): lax.psum_scatter((dot_transposed(row_block, qkv_flat) + first_back).astyp...  70.6 us
    all_gather x1, waiting for transfers between devices, body(): grad_out = lax.all_gather(cotangent, 'tensor', axis=0, tiled=True)  70.1 us
    all_gather x1, waiting for transfers between devices, body(): lax.all_gather(grad_middle.astype(jnp.bfloat16), 'tensor', axis=0, tiled=...  66.4 us
    all_gather x1, waiting for transfers between devices, body(): lax.all_gather(normed_mid_local.astype(jnp.bfloat16), 'tensor', axis=0, t...  63.8 us
    all_gather x1, waiting for transfers between devices, body(): arrived = lax.all_gather(sent_in, 'tensor', axis=0, tiled=True)  60.4 us
  transfers between devices with their start and end apart: 10, of which 10 were waited for; matrix products, arithmetic and copies ran while one was open for 12% of the time, Pallas kernels for 0%

commit v1 on v0

--- a/solution.py
+++ b/solution.py
@@ -12,6 +12,20 @@
 GELU_K = 0.044715
 NEGATIVE = -1e30
 EXACT_MODE = lax.Precision.HIGHEST
+
+
+def pair_rates(z_in):
+    later, val2 = (lax.axis_size("tensor"), lax.axis_index("tensor"))
+    h_now, b_next = (z_in, 1)
+    while b_next < later:
+        z2 = lax.ppermute(
+            h_now, axis_name="tensor", perm=[(j0, j0 ^ b_next) for j0 in range(later)]
+        )
+        main = jnp.concatenate([h_now, z2], axis=0)
+        block_next = jnp.concatenate([z2, h_now], axis=0)
+        h_now = jnp.where(val2 & b_next == 0, main, block_next)
+        b_next = 2 * b_next
+    return h_now
 
 
 def layer_norm(values, gain_row, shift_row):
@@ -288,7 +302,7 @@
     grad_middle = cotangent.astype(jnp.float32) + norm_back(
         grad_mid_norm, scaled_second, inverse_second, norm_gains[1]
     )
-    grad_mid_low = lax.all_gather(grad_middle.astype(jnp.bfloat16), "tensor", axis=0, tiled=True)
+    grad_mid_low = pair_rates(grad_middle.astype(jnp.bfloat16))
     grad_rank_ctx = low_rank_down(grad_mid_low, chosen_out_out)
     table_out_out = rank_grad(rank_ctx, grad_mid_low)
     table_out_in = rank_grad(grad_rank_ctx, attended_context)

time: 1050 us -> 1090 us (1.038)
  waiting for transfers between devices: 722 us -> 761 us
    ppermute x0 -> x2, waiting for transfers between devices: none -> 104 us  [pair_rates(): lax.ppermute(h_now, axis_name='tensor', perm=[(j0, j0 ^ b_next) for j0 in...]
    all_gather x1 -> x0, waiting for transfers between devices: 66.4 us -> none  [body(): lax.all_gather(grad_middle.astype(jnp.bfloat16), 'tensor', axis=0, tiled=...]
    unnamed x185 -> x197, local copies, waits for them, and re-layouts: 26.3 us -> 26.4 us
  transfers between devices with their start and end apart: 10 -> 11, of which waited for: 10 -> 11; matrix products, arithmetic and copies ran while one was open for 12% -> 11% of each run, Pallas kernels for 0% -> 0%
where the time goes in v1:
time: 1090 us; the launch traced here: 1080 us
  waiting for transfers between devices  761 us (70%)
  matrix products  200 us (18%)
  other arithmetic  59.5 us (5%)
  local copies, waits for them, and re-layouts  40 us (4%)
  between operations  16.5 us (2%)
    psum x1, waiting for transfers between devices, body(): lax.psum((to_tables(table_qkv_in, indicator_matrix[:, 0]), to_tables(tabl...  146 us
    ppermute x2, waiting for transfers between devices, pair_rates(): lax.ppermute(h_now, axis_name='tensor', perm=[(j0, j0 ^ b_next) for j0 in...  104 us
    reduce_scatter x1, waiting for transfers between devices, body(): lax.psum_scatter((jnp.dot(row_block, down_weight, preferred_element_type=...  77 us
    reduce_scatter x1, waiting for transfers between devices, body(): lax.psum_scatter((jnp.dot(row_block, output_weight, preferred_element_typ...  74.7 us
    all_gather x1, waiting for transfers between devices, body(): grad_out = lax.all_gather(cotangent, 'tensor', axis=0, tiled=True)  70.8 us
    reduce_scatter x1, waiting for transfers between devices, body(): lax.psum_scatter((dot_transposed(row_block, qkv_flat) + first_back).astyp...  70.6 us
    all_gather x1, waiting for transfers between devices, body(): lax.all_gather(normed_mid_local.astype(jnp.bfloat16), 'tensor', axis=0, t...  63.7 us
    all_gather x1, waiting for transfers between devices, body(): arrived = lax.all_gather(sent_in, 'tensor', axis=0, tiled=True)  60.2 us
  transfers between devices with their start and end apart: 11, of which 11 were waited for; matrix products, arithmetic and copies ran while one was open for 11% of the time, Pallas kernels for 0%

profile of v1, /device:TPU:0, one launch (start us, length us, event | category | flops | bytes accessed | tf_op | source)
XLA Modules:
  0.0 1082.3 jit_solution(13715077041143899116)
XLA Ops:
  17.7 9.0 copy.45
  38.3 60.2 %all-gather.4.cloned.1.call-done = bf16[1024,2048]{1,0:T(8,128)(2,1)} async-done(((bf16[256,2048]{1,0:T(8,128)(2,1)}), bf16[1024,2048]{1,0:T(8,128)(2,1)}) %all-gather.4.cloned.1.call-update) | async-done | bytes 4194320 | tf_op jit(solution)/shard_map/all_gather | solution.py:230
  102.0 8.8 fusion.114
  115.4 6.2 reshape.972
  151.8 5.6 add_convert_fusion.3
  158.2 74.7 %reduce-scatter.5.cloned.1.call-done = bf16[256,2048]{1,0:T(8,128)(2,1)} async-done(((bf16[1024,2048]{1,0:T(8,128)(2,1)}), bf16[256,2048]{1,0:T(8,128)(2,1)}) %reduce-scatter.5.cloned.1.call-update) | async-done | bytes 1048592 | tf_op jit(solution)/shard_map/reduce_scatter | solution.py:248
  245.0 70.8 %all-gather.8.cloned.1.call-done = bf16[1024,2048]{1,0:T(8,128)(2,1)} async-done(((bf16[256,2048]{1,0:T(8,128)(2,1)}), bf16[1024,2048]{1,0:T(8,128)(2,1)}) %all-gather.8.cloned.1.call-update) | async-done | bytes 4194320 | tf_op jit(solution)/shard_map/all_gather | solution.py:283
  320.0 13.5 %fusion.117 = f32[1024,2048]{1,0:T(8,128)} fusion(bf16[1024,2048]{1,0:T(8,128)(2,1)S(1)} %copy-done.13, bf16[2048,2048]{1,0:T(8,128)(2,1)} %param.32), kind=kOutput, calls=%fused_computation.209 | convolution fusion | flops 8589934592 | bytes 20971520 | tf_op jit(solution)/shard_map/dot_general | solution.py:57
  333.5 63.7 %all-gather.6.cloned.1.call-done = bf16[1024,2048]{1,0:T(8,128)(2,1)} async-done(((bf16[256,2048]{1,0:T(8,128)(2,1)}), bf16[1024,2048]{1,0:T(8,128)(2,1)}) %all-gather.6.cloned.1.call-update) | async-done | bytes 4194320 | tf_op jit(solution)/shard_map/all_gather | solution.py:260
  400.8 13.4 %fusion.115 = f32[1024,2048]{1,0:T(8,128)} fusion(bf16[1024,2048]{1,0:T(8,128)(2,1)S(1)} %copy-done.7, bf16[2048,2048]{1,0:T(8,128)(2,1)} %param.30), kind=kOutput, calls=%fused_computation.207 | convolution fusion | flops 8589934592 | bytes 20971520 | tf_op jit(solution)/shard_map/dot_general | solution.py:265
  414.2 10.2 multiply_convert_fusion.2
  424.3 11.4 %fusion.6 = bf16[1024,2048]{1,0:T(8,128)(2,1)S(1)} fusion(f32[1024,2048]{1,0:T(8,128)S(1)} %get-tuple-element.55, f32[1024,2048]{1,0:T(8,128)} %fusion.117, f32[16,1024]{1,0:T(8,128)S(1)} %copy-done.48, bf16[1,16,2048]{2,0,1:T(2,128)(2,1)S(1)} %fusion.51), kind=kOutput, calls=%fused_computation.8 | convolution fusion | flops 444596224 | bytes 21102592 | tf_op jit(solution)/shard_map/glr,grm->glm/dot_general | solution.py:75
  436.9 8.8 fusion.118
  455.8 11.5 %fusion.116 = f32[1024,2048]{1,0:T(8,128)S(1)} fusion(bf16[1024,2048]{1,0:T(8,128)(2,1)S(1)} %copy-done.11, bf16[2048,2048]{1,0:T(8,128)(2,1)} %param.32), kind=kOutput, calls=%fused_computation.208 | convolution fusion | flops 8589934592 | bytes 20971520 | tf_op jit(solution)/shard_map/dot_general | solution.py:275
  473.1 53.5 %reduce-scatter.9.cloned.1.call-done = bf16[256,2048]{1,0:T(8,128)(2,1)} async-done(((bf16[1024,2048]{1,0:T(8,128)(2,1)}), bf16[256,2048]{1,0:T(8,128)(2,1)}) %reduce-scatter.9.cloned.1.call-update) | async-done | bytes 1048592 | tf_op jit(solution)/shard_map/reduce_scatter | solution.py:296
  529.0 77.0 %reduce-scatter.7.cloned.1.call-done = bf16[256,2048]{1,0:T(8,128)(2,1)} async-done(((bf16[1024,2048]{1,0:T(8,128)(2,1)}), bf16[256,2048]{1,0:T(8,128)(2,1)}) %reduce-scatter.7.cloned.1.call-update) | async-done | bytes 1048592 | tf_op jit(solution)/shard_map/reduce_scatter | solution.py:274
  606.0 5.8 fusion.105
  613.4 23.6 %collective-permute-done = bf16[256,2048]{1,0:T(8,128)(2,1)} collective-permute-done((bf16[256,2048]{1,0:T(8,128)(2,1)}, bf16[256,2048]{1,0:T(8,128)(2,1)}, u32[]{:S(2)}, u32[]{:S(2)}) %collective-permute-start) | collective-permute-done | bytes 1048608 | tf_op jit(solution)/shard_map/ppermute | solution.py:21
  653.2 80.0 %collective-permute-done.1 = bf16[512,2048]{1,0:T(8,128)(2,1)S(1)} collective-permute-done((bf16[512,2048]{1,0:T(8,128)(2,1)S(1)}, bf16[512,2048]{1,0:T(8,128)(2,1)S(1)}, u32[]{:S(2)}, u32[]{:S(2)}) %collective-permute-start.1) | collective-permute-done | bytes 2097184 | tf_op jit(solution)/shard_map/ppermute | solution.py:21
  768.5 9.3 fusion.119
  781.9 7.5 add_convert_fusion
  799.0 40.1 %all-reduce.7.cloned.1.call-done = (bf16[8,16,3,512]{3,1,2,0:T(8,128)(2,1)}, bf16[8,16,512]{2,1,0:T(8,128)(2,1)}, bf16[8,16,2048]{2,1,0:T(8,128)(2,1)}, bf16[8,16,2048]{2,1,0:T(8,128)(2,1)}) async-done(((bf16[8,16,3,512]{3,1,2,0:T(8,128)(2,1)}, bf16[8,16,512]{2,1,0:T(8,128)(2,1)}, bf16[8,16,2048]{2,1,0:T(8,128)(2,1)}, bf16[8,16,2048]{2,1,0:T(8,128)(2,1)}), (bf16[8,16,3,512]{3,1,2,0:T(8,128)(2,1)}, ...) | async-done | bytes 1572880 | tf_op jit(solution)/shard_map/psum | solution.py:347
  846.9 70.6 %reduce-scatter.11.cloned.1.call-done = bf16[256,2048]{1,0:T(8,128)(2,1)} async-done(((bf16[1024,2048]{1,0:T(8,128)(2,1)}), bf16[256,2048]{1,0:T(8,128)(2,1)}) %reduce-scatter.11.cloned.1.call-update) | async-done | bytes 1048592 | tf_op jit(solution)/shard_map/reduce_scatter | solution.py:328
  923.1 145.9 %all-reduce.5.cloned.1.call-done = (f32[8,16,2048]{2,1,0:T(8,128)}, f32[8,16,2048]{2,1,0:T(8,128)}, f32[8,16,2048]{2,1,0:T(8,128)}, f32[8,16,2048]{2,1,0:T(8,128)}) async-done(((f32[8,16,2048]{2,1,0:T(8,128)}, f32[8,16,2048]{2,1,0:T(8,128)}, f32[8,16,2048]{2,1,0:T(8,128)}, f32[8,16,2048]{2,1,0:T(8,128)}), (f32[8,16,2048]{2,1,0:T(8,128)}, f32[8,16,2048]{2,1,0:T(8,128)}, f32[8,16,2048]{2,1,0:T(8,128)}, ...) | async-done | bytes 4194320 | tf_op jit(solution)/shard_map/psum | solution.py:337
  (318 shorter events, 184.7 us)
Async XLA Ops:
  7.2 142.1 %copy-start = (bf16[512,2048]{1,0:T(8,128)(2,1)S(1)}, bf16[512,2048]{1,0:T(8,128)(2,1)}, u32[]{:S(2)}) copy-start(bf16[512,2048]{1,0:T(8,128)(2,1)} %param.28) | copy-start | bytes 6291460
  7.2 91.3 %all-gather.4.cloned.1.call-start = ((), (), s32[]{:S(2)}) async-start(), calls=%async_computation.4 | async-start | bytes 5242880 | tf_op jit(solution)/shard_map/all_gather | solution.py:230
  14.9 218.0 %reduce-scatter.5.cloned.1.call-start = ((), (), s32[]{:S(2)}) async-start(), calls=%async_computation.5 | async-start | bytes 5242880 | tf_op jit(solution)/shard_map/reduce_scatter | solution.py:248
  31.8 210.0 %copy-start.54 = (bf16[1,4,8]{2,1,0:T(4,128)(2,1)}, bf16[1,4,8]{2,1,0:T(4,128)(2,1)S(1)}, u32[]{:S(2)}) copy-start(bf16[1,4,8]{2,1,0:T(4,128)(2,1)S(1)} %get-tuple-element.47) | copy-start | bytes 196
  32.0 117.1 %copy-start.55 = (bf16[1,16,512]{2,0,1:T(2,128)(2,1)}, bf16[1,16,512]{2,0,1:T(2,128)(2,1)S(1)}, u32[]{:S(2)}) copy-start(bf16[1,16,512]{2,0,1:T(2,128)(2,1)S(1)} %fusion.65) | copy-start | bytes 49156
  32.7 119.0 %copy-start.43 = (bf16[1,16,2048]{2,0,1:T(2,128)(2,1)}, bf16[1,16,2048]{2,0,1:T(2,128)(2,1)S(1)}, u32[]{:S(2)}) copy-start(bf16[1,16,2048]{2,0,1:T(2,128)(2,1)S(1)} %fusion.57) | copy-start | bytes 196612
  157.4 158.4 %all-gather.8.cloned.1.call-start = ((), (), s32[]{:S(2)}) async-start(), calls=%async_computation.8 | async-start | bytes 5242880 | tf_op jit(solution)/shard_map/all_gather | solution.py:283
  158.1 239.1 %all-gather.6.cloned.1.call-start = ((), (), s32[]{:S(2)}) async-start(), calls=%async_computation.6 | async-start | bytes 5242880 | tf_op jit(solution)/shard_map/all_gather | solution.py:260
  238.1 288.5 %reduce-scatter.9.cloned.1.call-start = ((), (), s32[]{:S(2)}) async-start(), calls=%async_computation.9 | async-start | bytes 5242880 | tf_op jit(solution)/shard_map/reduce_scatter | solution.py:296
  243.4 181.0 %copy-start.45 = (bf16[1,16,2048]{2,0,1:T(2,128)(2,1)}, bf16[1,16,2048]{2,0,1:T(2,128)(2,1)S(1)}, u32[]{:S(2)}) copy-start(bf16[1,16,2048]{2,0,1:T(2,128)(2,1)S(1)} %fusion.51) | copy-start | bytes 196612
  451.1 154.9 %reduce-scatter.7.cloned.1.call-start = ((), (), s32[]{:S(2)}) async-start(), calls=%async_computation.7 | async-start | bytes 5242880 | tf_op jit(solution)/shard_map/reduce_scatter | solution.py:274
  472.8 133.2 %copy-start.76 = (f32[2048]{0:T(1024)S(1)}, f32[2048]{0:T(1024)}, u32[]{:S(2)}) copy-start(f32[2048]{0:T(1024)} %param.33) | copy-start | bytes 24580
  472.9 366.2 %all-reduce.7.cloned.1.call-start = ((), (), s32[]{:S(2)}) async-start(), calls=%async_computation.12 | async-start | bytes 3145728 | tf_op jit(solution)/shard_map/psum | solution.py:347
  529.0 84.3 %copy-start.64 = (f32[4,512]{1,0:T(4,128)S(1)}, f32[4,512]{1,0:T(4,128)}, u32[]{:S(2)}) copy-start(f32[4,512]{1,0:T(4,128)} %copy-done.63) | copy-start | bytes 24580
  529.0 84.3 %copy-start.66 = (f32[4,512]{1,0:T(4,128)S(1)}, f32[4,512]{1,0:T(4,128)}, u32[]{:S(2)}) copy-start(f32[4,512]{1,0:T(4,128)} %copy-done.65) | copy-start | bytes 24580
  611.7 25.3 %collective-permute-start = (bf16[256,2048]{1,0:T(8,128)(2,1)}, bf16[256,2048]{1,0:T(8,128)(2,1)}, u32[]{:S(2)}, u32[]{:S(2)}) collective-permute-start(bf16[256,2048]{1,0:T(8,128)(2,1)} %get-tuple-element.22), channel_id=1, source_target_pairs={{0,1},{1,0},{2,3},{3,2},{4,5},{5,4},{6,7},{7,6},{8,9},{9,8},{10,11... | collective-permute-start | bytes 3145736 | tf_op jit(solution)/shard_map/ppermute | solution.py:21
  640.4 96.2 %copy-start.26 = (bf16[512,2048]{1,0:T(8,128)(2,1)}, bf16[512,2048]{1,0:T(8,128)(2,1)S(1)}, u32[]{:S(2)}) copy-start(bf16[512,2048]{1,0:T(8,128)(2,1)S(1)} %maximum_select_fusion.1) | copy-start | bytes 6291460
  640.4 92.8 %collective-permute-start.1 = (bf16[512,2048]{1,0:T(8,128)(2,1)S(1)}, bf16[512,2048]{1,0:T(8,128)(2,1)S(1)}, u32[]{:S(2)}, u32[]{:S(2)}) collective-permute-start(bf16[512,2048]{1,0:T(8,128)(2,1)S(1)} %maximum_select_fusion.1), channel_id=1, source_target_pairs={{0,2},{1,3},{2,0},{3,1},{4,6},{5,7},{6,4},{7,5},{8,10},{9,11},{10,... | collective-permute-start | bytes 6291464 | tf_op jit(solution)/shard_map/ppermute | solution.py:21
  648.7 84.5 %copy-start.44 = (bf16[1,16,2048]{2,0,1:T(2,128)(2,1)S(1)}, bf16[1,16,2048]{2,0,1:T(2,128)(2,1)}, u32[]{:S(2)}) copy-start(bf16[1,16,2048]{2,0,1:T(2,128)(2,1)} %copy-done.43) | copy-start | bytes 196612
  779.4 138.1 %reduce-scatter.11.cloned.1.call-start = ((), (), s32[]{:S(2)}) async-start(), calls=%async_computation.10 | async-start | bytes 5242880 | tf_op jit(solution)/shard_map/reduce_scatter | solution.py:328
  789.4 279.6 %all-reduce.5.cloned.1.call-start = ((), (), s32[]{:S(2)}) async-start(), calls=%async_computation.11 | async-start | bytes 8388608 | tf_op jit(solution)/shard_map/psum | solution.py:337
  798.9 118.6 %copy-start.52 = (f32[1,2048]{1,0:T(1,128)S(1)}, f32[1,2048]{1,0:T(1,128)}, u32[]{:S(2)}) copy-start(f32[1,2048]{1,0:T(1,128)} %copy-done.51) | copy-start | bytes 24580
  798.9 118.6 %copy-start.70 = (f32[256]{0:T(256)S(1)}, f32[256]{0:T(256)}, u32[]{:S(2)}) copy-start(f32[256]{0:T(256)} %copy-done.69) | copy-start | bytes 3076
  799.0 118.6 %copy-start.72 = (f32[256]{0:T(256)S(1)}, f32[256]{0:T(256)}, u32[]{:S(2)}) copy-start(f32[256]{0:T(256)} %copy-done.71) | copy-start | bytes 3076
  (82 other events, 1467.6 us)
Sparse Core Ops, SparseCore 0:
  15.0 83.4 all-gather.3
  157.5 75.2 reduce-scatter.4
  234.5 81.2 all-gather.7
  317.9 79.2 all-gather.5
  451.2 75.2 reduce-scatter.8
  528.7 77.2 reduce-scatter.6
  779.5 59.4 all-reduce.6
  841.3 76.1 reduce-scatter.10
  925.5 143.4 all-reduce.4
